TPU v7x, 1024 devices: a whole 4x4x32 slice. The times are simulated.
1024 devices in a mesh: section: 8 (over y, z_hi), dp: 4 (over x), tensor: 32 (over z_lo, core).
Axes of the slice: x: 4, y: 4, z: 32 (z_hi: 2, z_lo: 16; z = z_hi * 16 + z_lo), core: 2. Of those that a mesh axis runs over, the one named last changes fastest.
Arguments:
- cache: bfloat16 [8, 256, 5376], P('section'), may hold values from -6 to 6
- token_ids: int32 [128], replicated, may hold values from 0 to 255
- enc_weight: bfloat16 [8, 8192, 5376], P('section', ('dp', 'tensor')), may hold values from -0.078125 to 0.078125
- enc_bias: float32 [8, 8192], P('section', ('dp', 'tensor')), may hold values from -3 to 3
- dec_weight: bfloat16 [8, 8, 2688, 8192], P('section', None, ('dp', 'tensor')), may hold values from -0.25 to 0.25
- dec_bias: float32 [8, 2688], P('section', ('dp', 'tensor')), may hold values from -3 to 3
- incoming: float32 [8, 128, 2688], P('section', None, ('dp', 'tensor')), may hold values from -6 to 6
- target: bfloat16 [8, 128, 2688], P('section', None, ('dp', 'tensor')), may hold values from -6 to 6
- returned: bfloat16 [8, 128, 2688], P('section', None, ('dp', 'tensor')), may hold values from -6 to 6
Outputs:
- error: bfloat16 [8, 128, 2688], P('section', None, ('dp', 'tensor'))
- outgoing: float32 [8, 128, 2688], P('section', None, ('dp', 'tensor'))
- lat_grad: float32 [8, 8192, 128], P('section', ('dp', 'tensor'))
All inputs are finite; a program needn't handle non-finite values.
Results may differ from a plain program's by a relative error of at most 0.014.
Values may be sent and summed in bfloat16 or wider, within the bound.
A program may use at most 64 MiB of HBM per device.

v0:
```python
import jax
import jax.numpy as jnp
from jax import lax
from jax.sharding import PartitionSpec as P


def passed_along(shard, axis, by):
    length = lax.axis_size(axis)
    pairs = [(i, i + by) for i in range(length) if 0 <= i + by < length]
    return lax.ppermute(shard, axis, pairs)


def local(cache, token_ids, enc_weight, enc_bias, dec_weight, dec_bias, incoming, target, returned):
    layers = lax.axis_size("section")
    section = lax.axis_index("section")
    rows = jnp.take(cache[0], token_ids, axis=0)
    pre = lax.dot_general(
        rows, enc_weight[0], (((1,), (1,)), ((), ())), preferred_element_type=jnp.float32
    )
    latents = jnp.maximum(pre + enc_bias[0], 0.0).astype(jnp.bfloat16)
    decoders = dec_weight[0]
    tok_rows = latents.shape[0]
    columns = decoders.shape[1]
    block = decoders
    by_offset = jnp.einsum(
        "tn,kcn->ktc",
        lax.all_gather(latents, ("dp", "tensor"), axis=1, tiled=True),
        block,
        preferred_element_type=jnp.float32,
    )
    slot_ids = jnp.arange(layers)[:, None, None]
    placed = jnp.roll(by_offset, section, axis=0)
    within = jnp.where(slot_ids >= section, placed, 0.0)
    beyond = jnp.where(slot_ids < section, placed, 0.0)
    rising = jnp.zeros_like(within)
    falling = jnp.zeros_like(beyond)
    for step in range(layers - 1):
        rising = passed_along(rising + within, "section", 1)
        falling = passed_along((falling + beyond).astype(jnp.bfloat16), "section", -1).astype(
            jnp.float32
        )
    mine_in = lax.dynamic_index_in_dim(rising + within, section, 0, keepdims=True)
    mine_out = lax.dynamic_index_in_dim(falling + beyond, section, 0, keepdims=True)
    recon = mine_in + incoming + dec_bias[:, None, :]
    error = (recon - target.astype(jnp.float32)).astype(jnp.bfloat16)
    zero_slots = jnp.zeros((layers, tok_rows, columns), jnp.bfloat16)
    own_error = jnp.where(slot_ids == section, error, zero_slots)
    own_return = jnp.where(slot_ids == section, returned, zero_slots)
    lower = zero_slots
    higher = zero_slots
    for step in range(layers - 1):
        lower = passed_along(lower + own_error, "section", -1)
        higher = passed_along(higher + own_return, "section", 1)
    slots = jnp.where(slot_ids >= section, lower + own_error, higher)
    offsets = jnp.roll(slots, -section, axis=0)
    block = decoders
    lat_grad = lax.psum_scatter(
        jnp.einsum("kcn,ktc->nt", block, offsets, preferred_element_type=jnp.float32),
        ("dp", "tensor"),
        scatter_dimension=0,
        tiled=True,
    )
    return (error, mine_out, lat_grad[None])


def solution(mesh):
    placed = (
        P("section", None, None),
        P(),
        P("section", ("dp", "tensor"), None),
        P("section", ("dp", "tensor")),
        P("section", None, ("dp", "tensor"), None),
        P("section", ("dp", "tensor")),
        P("section", None, ("dp", "tensor")),
        P("section", None, ("dp", "tensor")),
        P("section", None, ("dp", "tensor")),
    )
    return jax.shard_map(
        local,
        mesh=mesh,
        in_specs=placed,
        out_specs=(
            P("section", None, ("dp", "tensor")),
            P("section", None, ("dp", "tensor")),
            P("section", ("dp", "tensor"), None),
        ),
        check_vma=False,
    )
```

profile of v0, /device:TPU:24, one launch (start us, length us, event | category | flops | bytes accessed | tf_op | source)
XLA Modules:
  0.0 2304.7 jit_solution(1019925940155270759)
XLA Ops:
  17.6 241.8 %all-gather.2.cloned.1.call-done = bf16[128,8192]{0,1:T(8,128)(2,1)} async-done(((bf16[128,64]{0,1:T(8,128)(2,1)}), bf16[128,8192]{0,1:T(8,128)(2,1)}) %all-gather.2.cloned.1.call-update) | async-done | bytes 2097168 | tf_op jit(solution)/shard_map/all_gather | solution.py:27
  262.9 13.8 collective-permute-start
  276.7 12.4 collective-permute-done
  289.1 12.8 collective-permute-start.1
  301.9 14.0 collective-permute-done.1
  315.9 11.1 collective-permute-start.2
  327.0 16.3 collective-permute-done.2
  351.9 17.2 collective-permute-done.3
  376.8 18.1 collective-permute-done.4
  401.9 18.9 collective-permute-done.5
  427.0 20.0 collective-permute-done.6
  447.1 15.8 collective-permute-start.14
  471.6 16.6 collective-permute-start.15
  496.1 17.4 collective-permute-start.16
  520.8 18.1 collective-permute-start.17
  545.7 18.5 collective-permute-start.18
  570.2 19.4 collective-permute-start.19
  597.4 23.4 %collective-permute-done.21 = bf16[8,128,21]{1,2,0:T(8,128)(2,1)S(1)} collective-permute-done((bf16[8,128,21]{1,2,0:T(8,128)(2,1)S(1)}, bf16[8,128,21]{1,2,0:T(8,128)(2,1)S(1)}, u32[]{:S(2)}, u32[]{:S(2)}) %collective-permute-start.21) | collective-permute-done | bytes 43040 | tf_op jit(solution)/shard_map/ppermute | solution.py:10
  622.8 23.3 %collective-permute-done.22 = bf16[8,128,21]{1,2,0:T(8,128)(2,1)S(1)} collective-permute-done((bf16[8,128,21]{1,2,0:T(8,128)(2,1)S(1)}, bf16[8,128,21]{1,2,0:T(8,128)(2,1)S(1)}, u32[]{:S(2)}, u32[]{:S(2)}) %collective-permute-start.22) | collective-permute-done | bytes 43040 | tf_op jit(solution)/shard_map/ppermute | solution.py:10
  648.1 23.9 %collective-permute-done.23 = bf16[8,128,21]{1,2,0:T(8,128)(2,1)S(1)} collective-permute-done((bf16[8,128,21]{1,2,0:T(8,128)(2,1)S(1)}, bf16[8,128,21]{1,2,0:T(8,128)(2,1)S(1)}, u32[]{:S(2)}, u32[]{:S(2)}) %collective-permute-start.23) | collective-permute-done | bytes 43040 | tf_op jit(solution)/shard_map/ppermute | solution.py:10
  674.1 23.3 %collective-permute-done.24 = bf16[8,128,21]{1,2,0:T(8,128)(2,1)S(1)} collective-permute-done((bf16[8,128,21]{1,2,0:T(8,128)(2,1)S(1)}, bf16[8,128,21]{1,2,0:T(8,128)(2,1)S(1)}, u32[]{:S(2)}, u32[]{:S(2)}) %collective-permute-start.24) | collective-permute-done | bytes 43040 | tf_op jit(solution)/shard_map/ppermute | solution.py:10
  699.4 23.3 %collective-permute-done.25 = bf16[8,128,21]{1,2,0:T(8,128)(2,1)S(1)} collective-permute-done((bf16[8,128,21]{1,2,0:T(8,128)(2,1)S(1)}, bf16[8,128,21]{1,2,0:T(8,128)(2,1)S(1)}, u32[]{:S(2)}, u32[]{:S(2)}) %collective-permute-start.25) | collective-permute-done | bytes 43040 | tf_op jit(solution)/shard_map/ppermute | solution.py:10
  724.7 23.1 %collective-permute-start.20 = (bf16[8,128,21]{1,2,0:T(8,128)(2,1)S(1)}, bf16[8,128,21]{1,2,0:T(8,128)(2,1)S(1)}, u32[]{:S(2)}, u32[]{:S(2)}) collective-permute-start(bf16[8,128,21]{1,2,0:T(8,128)(2,1)S(1)} %get-tuple-element.12), channel_id=1, source_target_pairs={{128,0},{256,128},{384,256},{512,384},{640,512},{768,640},{896,768... | collective-permute-start | bytes 129032 | tf_op jit(solution)/shard_map/ppermute | solution.py:10
  750.0 24.1 %collective-permute-done.27 = bf16[8,128,21]{1,2,0:T(8,128)(2,1)S(1)} collective-permute-done((bf16[8,128,21]{1,2,0:T(8,128)(2,1)S(1)}, bf16[8,128,21]{1,2,0:T(8,128)(2,1)S(1)}, u32[]{:S(2)}, u32[]{:S(2)}) %collective-permute-start.27) | collective-permute-done | bytes 43040 | tf_op jit(solution)/shard_map/ppermute | solution.py:10
  783.8 16.4 collective-permute-start.7
  808.2 18.0 collective-permute-start.8
  832.5 18.9 collective-permute-start.9
  856.9 19.9 collective-permute-start.10
  883.1 19.1 collective-permute-start.11
  908.4 19.2 collective-permute-start.12
  934.7 18.2 collective-permute-start.13
  960.2 1336.1 %reduce-scatter.4.cloned.1.call-done = f32[64,128]{1,0:T(8,128)} async-done(((f32[8192,128]{1,0:T(8,128)}), f32[64,128]{1,0:T(8,128)}) %reduce-scatter.4.cloned.1.call-update) | async-done | bytes 32784
  (86 shorter events, 157.7 us)
Async XLA Ops:
  7.2 252.3 %all-gather.2.cloned.1.call-start = ((), (), s32[]{:S(2)}) async-start(), calls=%async_computation.1 | async-start | bytes 2113536 | tf_op jit(solution)/shard_map/all_gather | solution.py:27
  17.5 2278.8 %reduce-scatter.4.cloned.1.call-start = ((), (), s32[]{:S(2)}) async-start(), calls=%async_computation.2 | async-start | bytes 4227072
  262.8 332.6 %copy-start.2 = (bf16[1,128,21]{1,2,0:T(8,128)(2,1)S(1)}, bf16[1,128,21]{1,2,0:T(8,128)(2,1)}, u32[]{:S(2)}) copy-start(bf16[1,128,21]{1,2,0:T(8,128)(2,1)} %param.17) | copy-start | bytes 16132
  262.9 26.2 %collective-permute-start = (f32[8,128,21]{1,2,0:T(8,128)S(1)}, f32[8,128,21]{1,2,0:T(8,128)S(1)}, u32[]{:S(2)}, u32[]{:S(2)}) collective-permute-start(f32[8,128,21]{1,2,0:T(8,128)S(1)} %get-tuple-element.11), channel_id=1, source_target_pairs={{0,128},{128,256},{256,384},{384,512},{512,640},{640,768},{768,896... | collective-permute-start | bytes 258056 | tf_op jit(solution)/shard_map/ppermute | solution.py:10
  289.1 26.8 %collective-permute-start.1 = (f32[8,128,21]{1,2,0:T(8,128)S(1)}, f32[8,128,21]{1,2,0:T(8,128)S(1)}, u32[]{:S(2)}, u32[]{:S(2)}) collective-permute-start(f32[8,128,21]{1,2,0:T(8,128)S(1)} %add.145), channel_id=1, source_target_pairs={{0,128},{128,256},{256,384},{384,512},{512,640},{640,768},{768,896... | collective-permute-start | bytes 258056 | tf_op jit(solution)/shard_map/ppermute | solution.py:10
  315.9 27.4 %collective-permute-start.2 = (f32[8,128,21]{1,2,0:T(8,128)S(1)}, f32[8,128,21]{1,2,0:T(8,128)S(1)}, u32[]{:S(2)}, u32[]{:S(2)}) collective-permute-start(f32[8,128,21]{1,2,0:T(8,128)S(1)} %add.146), channel_id=1, source_target_pairs={{0,128},{128,256},{256,384},{384,512},{512,640},{640,768},{768,896... | collective-permute-start | bytes 258056 | tf_op jit(solution)/shard_map/ppermute | solution.py:10
  343.3 25.8 %collective-permute-start.3 = (f32[8,128,21]{1,2,0:T(8,128)S(1)}, f32[8,128,21]{1,2,0:T(8,128)S(1)}, u32[]{:S(2)}, u32[]{:S(2)}) collective-permute-start(f32[8,128,21]{1,2,0:T(8,128)S(1)} %add.147), channel_id=1, source_target_pairs={{0,128},{128,256},{256,384},{384,512},{512,640},{640,768},{768,896... | collective-permute-start | bytes 258056 | tf_op jit(solution)/shard_map/ppermute | solution.py:10
  369.1 25.8 %collective-permute-start.4 = (f32[8,128,21]{1,2,0:T(8,128)S(1)}, f32[8,128,21]{1,2,0:T(8,128)S(1)}, u32[]{:S(2)}, u32[]{:S(2)}) collective-permute-start(f32[8,128,21]{1,2,0:T(8,128)S(1)} %add.148), channel_id=1, source_target_pairs={{0,128},{128,256},{256,384},{384,512},{512,640},{640,768},{768,896... | collective-permute-start | bytes 258056 | tf_op jit(solution)/shard_map/ppermute | solution.py:10
  395.0 25.8 %collective-permute-start.5 = (f32[8,128,21]{1,2,0:T(8,128)S(1)}, f32[8,128,21]{1,2,0:T(8,128)S(1)}, u32[]{:S(2)}, u32[]{:S(2)}) collective-permute-start(f32[8,128,21]{1,2,0:T(8,128)S(1)} %add.149), channel_id=1, source_target_pairs={{0,128},{128,256},{256,384},{384,512},{512,640},{640,768},{768,896... | collective-permute-start | bytes 258056 | tf_op jit(solution)/shard_map/ppermute | solution.py:10
  420.8 26.2 %collective-permute-start.6 = (f32[8,128,21]{1,2,0:T(8,128)S(1)}, f32[8,128,21]{1,2,0:T(8,128)S(1)}, u32[]{:S(2)}, u32[]{:S(2)}) collective-permute-start(f32[8,128,21]{1,2,0:T(8,128)S(1)} %add.150), channel_id=1, source_target_pairs={{0,128},{128,256},{256,384},{384,512},{512,640},{640,768},{768,896... | collective-permute-start | bytes 258056 | tf_op jit(solution)/shard_map/ppermute | solution.py:10
  447.0 331.2 %copy-start.1 = (bf16[1,128,21]{1,2,0:T(8,128)(2,1)}, bf16[1,128,21]{1,2,0:T(8,128)(2,1)S(1)}, u32[]{:S(2)}) copy-start(bf16[1,128,21]{1,2,0:T(8,128)(2,1)S(1)} %fusion.30) | copy-start | bytes 16132
  447.1 24.4 %collective-permute-start.14 = (bf16[8,128,21]{1,2,0:T(8,128)(2,1)S(1)}, bf16[8,128,21]{1,2,0:T(8,128)(2,1)S(1)}, u32[]{:S(2)}, u32[]{:S(2)}) collective-permute-start(bf16[8,128,21]{1,2,0:T(8,128)(2,1)S(1)} %broadcast_select_fusion.3), channel_id=1, source_target_pairs={{128,0},{256,128},{384,256},{512,384},{640,512},{768,640},{896,768... | collective-permute-start | bytes 129032 | tf_op jit(solution)/shard_map/ppermute | solution.py:10
  471.6 24.4 %collective-permute-start.15 = (bf16[8,128,21]{1,2,0:T(8,128)(2,1)S(1)}, bf16[8,128,21]{1,2,0:T(8,128)(2,1)S(1)}, u32[]{:S(2)}, u32[]{:S(2)}) collective-permute-start(bf16[8,128,21]{1,2,0:T(8,128)(2,1)S(1)} %select_add_fusion.6), channel_id=1, source_target_pairs={{128,0},{256,128},{384,256},{512,384},{640,512},{768,640},{896,768... | collective-permute-start | bytes 129032 | tf_op jit(solution)/shard_map/ppermute | solution.py:10
  496.1 24.6 %collective-permute-start.16 = (bf16[8,128,21]{1,2,0:T(8,128)(2,1)S(1)}, bf16[8,128,21]{1,2,0:T(8,128)(2,1)S(1)}, u32[]{:S(2)}, u32[]{:S(2)}) collective-permute-start(bf16[8,128,21]{1,2,0:T(8,128)(2,1)S(1)} %select_add_fusion.5), channel_id=1, source_target_pairs={{128,0},{256,128},{384,256},{512,384},{640,512},{768,640},{896,768... | collective-permute-start | bytes 129032 | tf_op jit(solution)/shard_map/ppermute | solution.py:10
  520.8 24.8 %collective-permute-start.17 = (bf16[8,128,21]{1,2,0:T(8,128)(2,1)S(1)}, bf16[8,128,21]{1,2,0:T(8,128)(2,1)S(1)}, u32[]{:S(2)}, u32[]{:S(2)}) collective-permute-start(bf16[8,128,21]{1,2,0:T(8,128)(2,1)S(1)} %select_add_fusion.4), channel_id=1, source_target_pairs={{128,0},{256,128},{384,256},{512,384},{640,512},{768,640},{896,768... | collective-permute-start | bytes 129032 | tf_op jit(solution)/shard_map/ppermute | solution.py:10
  545.7 24.4 %collective-permute-start.18 = (bf16[8,128,21]{1,2,0:T(8,128)(2,1)S(1)}, bf16[8,128,21]{1,2,0:T(8,128)(2,1)S(1)}, u32[]{:S(2)}, u32[]{:S(2)}) collective-permute-start(bf16[8,128,21]{1,2,0:T(8,128)(2,1)S(1)} %select_add_fusion.3), channel_id=1, source_target_pairs={{128,0},{256,128},{384,256},{512,384},{640,512},{768,640},{896,768... | collective-permute-start | bytes 129032 | tf_op jit(solution)/shard_map/ppermute | solution.py:10
  570.2 25.2 %collective-permute-start.19 = (bf16[8,128,21]{1,2,0:T(8,128)(2,1)S(1)}, bf16[8,128,21]{1,2,0:T(8,128)(2,1)S(1)}, u32[]{:S(2)}, u32[]{:S(2)}) collective-permute-start(bf16[8,128,21]{1,2,0:T(8,128)(2,1)S(1)} %select_add_fusion.2), channel_id=1, source_target_pairs={{128,0},{256,128},{384,256},{512,384},{640,512},{768,640},{896,768... | collective-permute-start | bytes 129032 | tf_op jit(solution)/shard_map/ppermute | solution.py:10
  595.5 25.3 %collective-permute-start.21 = (bf16[8,128,21]{1,2,0:T(8,128)(2,1)S(1)}, bf16[8,128,21]{1,2,0:T(8,128)(2,1)S(1)}, u32[]{:S(2)}, u32[]{:S(2)}) collective-permute-start(bf16[8,128,21]{1,2,0:T(8,128)(2,1)S(1)} %get-tuple-element.13), channel_id=1, source_target_pairs={{0,128},{128,256},{256,384},{384,512},{512,640},{640,768},{768,896... | collective-permute-start | bytes 129032 | tf_op jit(solution)/shard_map/ppermute | solution.py:10
  620.9 25.2 %collective-permute-start.22 = (bf16[8,128,21]{1,2,0:T(8,128)(2,1)S(1)}, bf16[8,128,21]{1,2,0:T(8,128)(2,1)S(1)}, u32[]{:S(2)}, u32[]{:S(2)}) collective-permute-start(bf16[8,128,21]{1,2,0:T(8,128)(2,1)S(1)} %select_add_fusion.12), channel_id=1, source_target_pairs={{0,128},{128,256},{256,384},{384,512},{512,640},{640,768},{768,896... | collective-permute-start | bytes 129032 | tf_op jit(solution)/shard_map/ppermute | solution.py:10
  646.2 25.9 %collective-permute-start.23 = (bf16[8,128,21]{1,2,0:T(8,128)(2,1)S(1)}, bf16[8,128,21]{1,2,0:T(8,128)(2,1)S(1)}, u32[]{:S(2)}, u32[]{:S(2)}) collective-permute-start(bf16[8,128,21]{1,2,0:T(8,128)(2,1)S(1)} %select_add_fusion.11), channel_id=1, source_target_pairs={{0,128},{128,256},{256,384},{384,512},{512,640},{640,768},{768,896... | collective-permute-start | bytes 129032 | tf_op jit(solution)/shard_map/ppermute | solution.py:10
  672.1 25.2 %collective-permute-start.24 = (bf16[8,128,21]{1,2,0:T(8,128)(2,1)S(1)}, bf16[8,128,21]{1,2,0:T(8,128)(2,1)S(1)}, u32[]{:S(2)}, u32[]{:S(2)}) collective-permute-start(bf16[8,128,21]{1,2,0:T(8,128)(2,1)S(1)} %select_add_fusion.10), channel_id=1, source_target_pairs={{0,128},{128,256},{256,384},{384,512},{512,640},{640,768},{768,896... | collective-permute-start | bytes 129032 | tf_op jit(solution)/shard_map/ppermute | solution.py:10
  697.4 25.2 %collective-permute-start.25 = (bf16[8,128,21]{1,2,0:T(8,128)(2,1)S(1)}, bf16[8,128,21]{1,2,0:T(8,128)(2,1)S(1)}, u32[]{:S(2)}, u32[]{:S(2)}) collective-permute-start(bf16[8,128,21]{1,2,0:T(8,128)(2,1)S(1)} %select_add_fusion.9), channel_id=1, source_target_pairs={{0,128},{128,256},{256,384},{384,512},{512,640},{640,768},{768,896... | collective-permute-start | bytes 129032 | tf_op jit(solution)/shard_map/ppermute | solution.py:10
  722.7 25.2 %collective-permute-start.26 = (bf16[8,128,21]{1,2,0:T(8,128)(2,1)S(1)}, bf16[8,128,21]{1,2,0:T(8,128)(2,1)S(1)}, u32[]{:S(2)}, u32[]{:S(2)}) collective-permute-start(bf16[8,128,21]{1,2,0:T(8,128)(2,1)S(1)} %select_add_fusion.8), channel_id=1, source_target_pairs={{0,128},{128,256},{256,384},{384,512},{512,640},{640,768},{768,896... | collective-permute-start | bytes 129032 | tf_op jit(solution)/shard_map/ppermute | solution.py:10
  724.7 25.3 %collective-permute-start.20 = (bf16[8,128,21]{1,2,0:T(8,128)(2,1)S(1)}, bf16[8,128,21]{1,2,0:T(8,128)(2,1)S(1)}, u32[]{:S(2)}, u32[]{:S(2)}) collective-permute-start(bf16[8,128,21]{1,2,0:T(8,128)(2,1)S(1)} %get-tuple-element.12), channel_id=1, source_target_pairs={{128,0},{256,128},{384,256},{512,384},{640,512},{768,640},{896,768... | collective-permute-start | bytes 129032 | tf_op jit(solution)/shard_map/ppermute | solution.py:10
  748.0 26.0 %collective-permute-start.27 = (bf16[8,128,21]{1,2,0:T(8,128)(2,1)S(1)}, bf16[8,128,21]{1,2,0:T(8,128)(2,1)S(1)}, u32[]{:S(2)}, u32[]{:S(2)}) collective-permute-start(bf16[8,128,21]{1,2,0:T(8,128)(2,1)S(1)} %select_add_fusion.7), channel_id=1, source_target_pairs={{0,128},{128,256},{256,384},{384,512},{512,640},{640,768},{768,896... | collective-permute-start | bytes 129032 | tf_op jit(solution)/shard_map/ppermute | solution.py:10
  783.8 24.3 %collective-permute-start.7 = (bf16[8,128,21]{1,2,0:T(8,128)(2,1)S(1)}, bf16[8,128,21]{1,2,0:T(8,128)(2,1)S(1)}, u32[]{:S(2)}, u32[]{:S(2)}) collective-permute-start(bf16[8,128,21]{1,2,0:T(8,128)(2,1)S(1)} %get-tuple-element.9), channel_id=1, source_target_pairs={{128,0},{256,128},{384,256},{512,384},{640,512},{768,640},{896,768... | collective-permute-start | bytes 129032 | tf_op jit(solution)/shard_map/ppermute | solution.py:10
  808.2 24.3 %collective-permute-start.8 = (bf16[8,128,21]{1,2,0:T(8,128)(2,1)S(1)}, bf16[8,128,21]{1,2,0:T(8,128)(2,1)S(1)}, u32[]{:S(2)}, u32[]{:S(2)}) collective-permute-start(bf16[8,128,21]{1,2,0:T(8,128)(2,1)S(1)} %add_convert_fusion.5), channel_id=1, source_target_pairs={{128,0},{256,128},{384,256},{512,384},{640,512},{768,640},{896,768... | collective-permute-start | bytes 129032 | tf_op jit(solution)/shard_map/ppermute | solution.py:10
  832.5 24.4 %collective-permute-start.9 = (bf16[8,128,21]{1,2,0:T(8,128)(2,1)S(1)}, bf16[8,128,21]{1,2,0:T(8,128)(2,1)S(1)}, u32[]{:S(2)}, u32[]{:S(2)}) collective-permute-start(bf16[8,128,21]{1,2,0:T(8,128)(2,1)S(1)} %add_convert_fusion.4), channel_id=1, source_target_pairs={{128,0},{256,128},{384,256},{512,384},{640,512},{768,640},{896,768... | collective-permute-start | bytes 129032 | tf_op jit(solution)/shard_map/ppermute | solution.py:10
  856.9 26.2 %collective-permute-start.10 = (bf16[8,128,21]{1,2,0:T(8,128)(2,1)S(1)}, bf16[8,128,21]{1,2,0:T(8,128)(2,1)S(1)}, u32[]{:S(2)}, u32[]{:S(2)}) collective-permute-start(bf16[8,128,21]{1,2,0:T(8,128)(2,1)S(1)} %add_convert_fusion.3), channel_id=1, source_target_pairs={{128,0},{256,128},{384,256},{512,384},{640,512},{768,640},{896,768... | collective-permute-start | bytes 129032 | tf_op jit(solution)/shard_map/ppermute | solution.py:10
  883.1 25.3 %collective-permute-start.11 = (bf16[8,128,21]{1,2,0:T(8,128)(2,1)S(1)}, bf16[8,128,21]{1,2,0:T(8,128)(2,1)S(1)}, u32[]{:S(2)}, u32[]{:S(2)}) collective-permute-start(bf16[8,128,21]{1,2,0:T(8,128)(2,1)S(1)} %add_convert_fusion.2), channel_id=1, source_target_pairs={{128,0},{256,128},{384,256},{512,384},{640,512},{768,640},{896,768... | collective-permute-start | bytes 129032 | tf_op jit(solution)/shard_map/ppermute | solution.py:10
  908.4 26.3 %collective-permute-start.12 = (bf16[8,128,21]{1,2,0:T(8,128)(2,1)S(1)}, bf16[8,128,21]{1,2,0:T(8,128)(2,1)S(1)}, u32[]{:S(2)}, u32[]{:S(2)}) collective-permute-start(bf16[8,128,21]{1,2,0:T(8,128)(2,1)S(1)} %add_convert_fusion.1), channel_id=1, source_target_pairs={{128,0},{256,128},{384,256},{512,384},{640,512},{768,640},{896,768... | collective-permute-start | bytes 129032 | tf_op jit(solution)/shard_map/ppermute | solution.py:10
  934.7 24.9 %collective-permute-start.13 = (bf16[8,128,21]{1,2,0:T(8,128)(2,1)S(1)}, bf16[8,128,21]{1,2,0:T(8,128)(2,1)S(1)}, u32[]{:S(2)}, u32[]{:S(2)}) collective-permute-start(bf16[8,128,21]{1,2,0:T(8,128)(2,1)S(1)} %add_convert_fusion), channel_id=1, source_target_pairs={{128,0},{256,128},{384,256},{512,384},{640,512},{768,640},{896,768... | collective-permute-start | bytes 129032 | tf_op jit(solution)/shard_map/ppermute | solution.py:10
  (5 other events, 820.8 us)
Sparse Core Ops, SparseCore 0:
  17.6 241.7 all-gather.1
  784.0 1512.2 reduce-scatter.3
where the time goes:
time: 2310 us; the launch traced here: 2300 us
  waiting for transfers between devices  1920 us (83%)
  starting transfers between devices  339 us (15%)
    unnamed x3, waiting for transfers between devices  1340 us
    ppermute x28, waiting for transfers between devices, passed_along(): return lax.ppermute(shard, axis, pairs)  346 us
    ppermute x28, starting transfers between devices, passed_along(): return lax.ppermute(shard, axis, pairs)  339 us
    all_gather x1, waiting for transfers between devices, local(): lax.all_gather(latents, ('dp', 'tensor'), axis=1, tiled=True)  242 us
  transfers between devices with their start and end apart: 30, of which 29 were waited for; matrix products, arithmetic and copies ran while one was open for 0% of the time, Pallas kernels for 0%

commit v1 on v0

v1 whole, which is shorter than its diff:
```python
import functools

import jax
import jax.numpy as jnp
from jax import lax
from jax.experimental import pallas as pl
from jax.experimental.pallas import tpu as pltpu
from jax.sharding import PartitionSpec as P

MESH = pl.DeviceIdType.MESH
F32 = jnp.float32
BF16 = jnp.bfloat16
FEAT = 24
ORDER = (1, 3, 2)


class Links:
    def __init__(self, send, recv):
        self.send, self.recv, self.used, self.open = send, recv, 0, []

    def message(self):
        self.used += 1
        return self.used - 1

    def copy(self, index, src, dst, peer):
        return pltpu.make_async_remote_copy(
            src_ref=src,
            dst_ref=dst,
            send_sem=self.send.at[index],
            recv_sem=self.recv.at[index],
            device_id=peer,
            device_id_type=MESH,
        )

    def start(self, index, src, dst, peer):
        copy = self.copy(index, src, dst, peer)
        copy.start()
        self.open.append(copy)

    def arrived(self, index, dst, peer):
        self.copy(index, dst, dst, peer).wait_recv()

    def drain(self):
        for copy in self.open:
            copy.wait_send()


MESSAGES = 112


def column_of(row, rows):
    n = row.shape[1]
    down = lax.broadcasted_iota(jnp.int32, (rows, n), 0)
    along = lax.broadcasted_iota(jnp.int32, (rows, n), 1)
    return jnp.sum(jnp.where(down == along, row, 0.0), axis=1, keepdims=True)


def kernel(
    tok, ebias, dbias, inc, tgt, ret, cache_h, enc_h, w_h,
    err_o, out_o, lg_o,
    cache_v, enc_v, w_v, lat, pbuf, rc, qbuf, rx, ub, rb, vf, vb, ra,
    cacc, bk, ysend, yrecv, zsend, zrecv, osend, orecv, esend, erecv,
    rsend, rrecv, gsend, grecv, load, send, recv,
):
    s, d, t = lax.axis_index("section"), lax.axis_index("dp"), lax.axis_index("tensor")
    y, zh, x, z, c = s // 2, s % 2, d, t // 2, t % 2
    zg, zp = z // 4, z % 4
    core_peer = (s, d, z * 2 + 1 - c)
    x_peer = lambda k: (s, (x + k) % 4, t)
    a_peer = lambda k: (s, d, (((zg + k) % 4) * 4 + zp) * 2 + c)
    b_peer = lambda k: (s, d, (zg * 4 + (zp + k) % 4) * 2 + c)
    y_peer = lambda k: (((y + k) % 4) * 2 + zh, d, t)
    z_peer = (y * 2 + 1 - zh, d, t)

    barrier = pltpu.get_barrier_semaphore()
    peers = [z_peer, core_peer]
    for k in (1, 2, 3):
        peers += [a_peer(k), b_peer(k), x_peer(k), y_peer(k)]
    for peer in peers:
        pl.semaphore_signal(barrier, inc=1, device_id=peer, device_id_type=MESH)

    loads = [
        pltpu.make_async_copy(cache_h, cache_v, load.at[0]),
        pltpu.make_async_copy(enc_h, enc_v, load.at[1]),
        pltpu.make_async_copy(w_h, w_v, load.at[2]),
    ]
    for one in loads:
        one.start()
    links = Links(send, recv)

    rows_of = lax.broadcasted_iota(jnp.int32, (256, 128), 0)
    pick = jnp.where(rows_of == tok[...], 1.0, 0.0).astype(BF16)
    bias = column_of(ebias[...], 64)
    loads[0].wait()
    loads[1].wait()
    pre = lax.dot_general(
        enc_v[...], cache_v[...], (((1,), (1,)), ((), ())), preferred_element_type=F32
    )
    every = jnp.maximum(pre + bias, 0.0).astype(BF16)
    mine = jnp.dot(every, pick, preferred_element_type=F32).astype(BF16)
    lat[x, zp, zg, c] = mine

    pl.semaphore_wait(barrier, len(peers))

    m_a = {k: links.message() for k in (1, 2, 3)}
    m_b = {(k, j): links.message() for k in (1, 2, 3) for j in range(4)}
    m_x = {(k, g): links.message() for k in (1, 2, 3) for g in range(4)}
    m_c = {(k, g): links.message() for k in range(4) for g in range(4)}
    for k in ORDER:
        here = lat.at[x, zp, zg, c]
        links.start(m_a[k], here, here, a_peer(k))
    for k in ORDER:
        here = lat.at[x, zp, zg, c]
        links.start(m_b[k, 0], here, here, b_peer(k))

    zero_rows = jnp.zeros((FEAT - 21, 128), F32)
    returned = jnp.concatenate([ret[...].astype(F32), zero_rows], axis=0)
    rsend[...] = jnp.concatenate([returned, jnp.zeros((8, 128), F32)], axis=0).astype(BF16)
    m_r = links.message()
    links.start(m_r, rsend, rrecv, z_peer)

    for j in ORDER:
        from_a = lat.at[x, zp, (zg - j + 4) % 4, c]
        links.arrived(m_a[j], from_a, a_peer(j))
        for k in ORDER:
            links.start(m_b[k, j], from_a, from_a, b_peer(k))

    def group(k, g):
        return lat.at[(x - k + 4) % 4, (zp - g + 4) % 4, :, c]

    def pass_on(g):
        for k in ORDER:
            links.start(m_x[k, g], group(0, g), group(0, g), x_peer(k))
        links.start(m_c[0, g], group(0, g), group(0, g), core_peer)

    def weights(x_at, zp_at):
        cut = []
        for q in range(4):
            first = pl.multiple_of((x_at * 16 + q * 4 + zp_at) * 128, 128)
            cut.append(w_v[:, pl.ds(first, 128)])
        return jnp.concatenate(cut, axis=1)

    def decode(k, g):
        x_at, zp_at = (x - k + 4) % 4, (zp - g + 4) % 4
        links.arrived(m_c[k, g], lat.at[x_at, zp_at, :, 1 - c], core_peer)
        block = lat[x_at, zp_at].reshape(512, 128)
        cacc[0:168] += jnp.dot(weights(x_at, zp_at), block, preferred_element_type=F32)

    cacc[...] = jnp.zeros_like(cacc)
    loads[2].wait()
    sequence = (0,) + ORDER
    done = []
    for at, g in enumerate(sequence):
        if g > 0:
            for j in range(4):
                from_b = lat.at[x, (zp - g + 4) % 4, (zg - j + 4) % 4, c]
                links.arrived(m_b[g, j], from_b, b_peer(g))
        pass_on(g)
        if at > 0:
            before = sequence[at - 1]
            for k in ORDER:
                links.arrived(m_x[k, before], group(k, before), x_peer(k))
                links.start(m_c[k, before], group(k, before), group(k, before), core_peer)
            if at > 1:
                for k in range(4):
                    decode(k, sequence[at - 2])
    last = sequence[3]
    for k in range(4):
        decode(k, sequence[2])
    decode(0, last)
    for k in ORDER:
        links.arrived(m_x[k, last], group(k, last), x_peer(k))
        links.start(m_c[k, last], group(k, last), group(k, last), core_peer)

    links.arrived(m_r, rrecv, z_peer)
    gsend[...] = jnp.concatenate([returned, rrecv[...].astype(F32)[:FEAT]], axis=0).astype(BF16)
    m_g = {k: links.message() for k in (1, 2, 3)}
    for k in ORDER:
        links.start(m_g[k], gsend, grecv.at[k - 1], y_peer(k))
    for k in ORDER:
        decode(k, last)

    def piece(offset):
        return cacc[pl.ds(offset, FEAT, stride=8), :]

    cross_of = lambda dy: (2 * dy + 1 - 2 * zh + 8) % 8
    m_y = {k: links.message() for k in (1, 2, 3)}
    for k in ORDER:
        ysend[k - 1] = jnp.concatenate([piece(2 * k), piece(cross_of(k))], axis=0).astype(BF16)
        links.start(m_y[k], ysend.at[k - 1], yrecv.at[k - 1], y_peer(k))
    base = inc[...].reshape(21, 128) + column_of(dbias[...], 21) - tgt[...].astype(F32)
    base = jnp.concatenate([base, zero_rows], axis=0)
    own_cross = piece(cross_of(0))
    e_same = base + piece(0)
    o_same = jnp.zeros((FEAT, 128), F32)
    e_cross = jnp.where(zh == 0, own_cross, 0.0)
    o_cross = jnp.where(zh == 0, 0.0, own_cross)
    for k in ORDER:
        links.arrived(m_y[k], yrecv.at[k - 1], y_peer(k))
        both = yrecv[k - 1].astype(F32)
        same, cross = both[:FEAT], both[FEAT:]
        e_same += jnp.where(y >= k, same, 0.0)
        o_same += jnp.where(y >= k, 0.0, same)
        e_cross += jnp.where(y >= k, cross, 0.0)
        o_cross += jnp.where(y >= k, 0.0, cross)
    m_z, m_o = links.message(), links.message()
    zsend[...] = jnp.concatenate([e_same, e_cross], axis=0).astype(BF16)
    links.start(m_z, zsend, zrecv, z_peer)
    osend[...] = jnp.concatenate([o_cross, jnp.zeros((8, 128), F32)], axis=0).astype(BF16)
    links.start(m_o, osend, orecv, z_peer)
    links.arrived(m_z, zrecv, z_peer)
    both = zrecv[...].astype(F32)
    mine_err = e_same + both[FEAT:]
    other_err = e_cross + both[:FEAT]
    esend[...] = jnp.concatenate([mine_err, other_err], axis=0).astype(BF16)
    m_e = {k: links.message() for k in (1, 2, 3)}
    for k in ORDER:
        links.start(m_e[k], esend, erecv.at[k - 1], y_peer(k))
    err_o[...] = mine_err[:21].astype(BF16)

    for dy in range(4):
        k = (4 - dy) % 4
        if k == 0:
            mine_b, ret_b = esend[...].astype(F32), gsend[...].astype(F32)
            same = mine_b[:FEAT]
            cross = jnp.where(zh == 0, mine_b[FEAT:], ret_b[FEAT:])
        else:
            links.arrived(m_g[k], grecv.at[k - 1], y_peer(k))
            links.arrived(m_e[k], erecv.at[k - 1], y_peer(k))
            mine_b, ret_b = erecv[k - 1].astype(F32), grecv[k - 1].astype(F32)
            both = jnp.where(y + dy < 4, mine_b, ret_b)
            same, cross = both[:FEAT], both[FEAT:]
        bk[pl.ds(2 * dy, FEAT, stride=8), :] = same
        bk[pl.ds(cross_of(dy), FEAT, stride=8), :] = cross
    back = bk[0:168].astype(BF16)

    n_c = {(k, g): links.message() for k in range(4) for g in range(4)}
    n_x = {(k, g): links.message() for k in (1, 2, 3) for g in range(4)}
    n_b = {g: links.message() for g in (1, 2, 3)}
    n_a = {j: links.message() for j in (1, 2, 3)}

    def gradient(k, g):
        x_at, zp_at = (x + k) % 4, (zp + g) % 4
        part = lax.dot_general(
            weights(x_at, zp_at), back, (((0,), (0,)), ((), ())), preferred_element_type=F32
        )
        pbuf[x_at, zp_at] = part.astype(BF16).reshape(4, 2, 64, 128)
        links.start(n_c[k, g], pbuf.at[x_at, zp_at, :, 1 - c], rc.at[k, g], core_peer)

    def chip_sum(k, g):
        x_at, zp_at = (x + k) % 4, (zp + g) % 4
        links.arrived(n_c[k, g], rc.at[k, g], core_peer)
        total = pbuf[x_at, zp_at, :, c].astype(F32) + rc[k, g].astype(F32)
        qbuf[k, g] = total.astype(BF16)
        if k > 0:
            links.start(n_x[k, g], qbuf.at[k, g], rx.at[k - 1, g], x_peer(k))

    def row_sum(g):
        total = qbuf[0, g].astype(F32)
        for k in ORDER:
            links.arrived(n_x[k, g], rx.at[k - 1, g], x_peer(k))
            total += rx[k - 1, g].astype(F32)
        if g > 0:
            ub[g - 1] = total.astype(BF16)
            links.start(n_b[g], ub.at[g - 1], rb.at[g - 1], b_peer(g))
        else:
            vf[...] = total

    steps = [(k, g) for g in ORDER + (0,) for k in ORDER + (0,)]
    for at, step in enumerate(steps):
        gradient(*step)
        if at >= 2:
            chip_sum(*steps[at - 2])
    chip_sum(*steps[-2])
    chip_sum(*steps[-1])
    links.arrived(m_o, orecv, z_peer)
    outgoing = o_same + orecv[...].astype(F32)[:FEAT]
    out_o[...] = outgoing[:21].reshape(21, 1, 128)
    for g in ORDER + (0,):
        row_sum(g)
    total = vf[...]
    for g in ORDER:
        links.arrived(n_b[g], rb.at[g - 1], b_peer(g))
        total += rb[g - 1].astype(F32)
    vf[...] = total
    vb[...] = total.astype(BF16)
    for j in ORDER:
        links.start(n_a[j], vb.at[(zg + j) % 4], ra.at[j - 1], a_peer(j))
    total = vf[zg]
    for j in ORDER:
        links.arrived(n_a[j], ra.at[j - 1], a_peer(j))
        total += ra[j - 1].astype(F32)
    lg_o[...] = total
    links.drain()


def local(cache, token_ids, enc_weight, enc_bias, dec_weight, dec_bias, incoming, target, returned):
    whole = pl.BlockSpec(memory_space=pltpu.VMEM)
    left = pl.BlockSpec(memory_space=pl.ANY)
    weights = jnp.transpose(dec_weight[0], (1, 0, 2)).reshape(168, 8192)
    err, out, grad = pl.pallas_call(
        kernel,
        out_shape=(
            jax.ShapeDtypeStruct((21, 128), BF16),
            jax.ShapeDtypeStruct((21, 1, 128), F32),
            jax.ShapeDtypeStruct((64, 128), F32),
        ),
        in_specs=[whole] * 6 + [left] * 3,
        out_specs=(whole, whole, whole),
        scratch_shapes=[
            pltpu.VMEM((256, 5376), BF16),
            pltpu.VMEM((64, 5376), BF16),
            pltpu.VMEM((168, 8192), BF16),
            pltpu.VMEM((4, 4, 4, 2, 64, 128), BF16),
            pltpu.VMEM((4, 4, 4, 2, 64, 128), BF16),
            pltpu.VMEM((4, 4, 4, 64, 128), BF16),
            pltpu.VMEM((4, 4, 4, 64, 128), BF16),
            pltpu.VMEM((3, 4, 4, 64, 128), BF16),
            pltpu.VMEM((3, 4, 64, 128), BF16),
            pltpu.VMEM((3, 4, 64, 128), BF16),
            pltpu.VMEM((4, 64, 128), F32),
            pltpu.VMEM((4, 64, 128), BF16),
            pltpu.VMEM((3, 64, 128), BF16),
            pltpu.VMEM((192, 128), F32),
            pltpu.VMEM((192, 128), F32),
            pltpu.VMEM((3, 48, 128), BF16),
            pltpu.VMEM((3, 48, 128), BF16),
            pltpu.VMEM((48, 128), BF16),
            pltpu.VMEM((48, 128), BF16),
            pltpu.VMEM((32, 128), BF16),
            pltpu.VMEM((32, 128), BF16),
            pltpu.VMEM((48, 128), BF16),
            pltpu.VMEM((3, 48, 128), BF16),
            pltpu.VMEM((32, 128), BF16),
            pltpu.VMEM((32, 128), BF16),
            pltpu.VMEM((48, 128), BF16),
            pltpu.VMEM((3, 48, 128), BF16),
            pltpu.SemaphoreType.DMA((3,)),
            pltpu.SemaphoreType.DMA((MESSAGES,)),
            pltpu.SemaphoreType.DMA((MESSAGES,)),
        ],
        compiler_params=pltpu.CompilerParams(
            collective_id=0, has_side_effects=True, vmem_limit_bytes=48 << 20
        ),
        name="transcoder",
    )(
        token_ids.reshape(1, 128),
        enc_bias,
        dec_bias,
        jnp.transpose(incoming, (2, 0, 1)),
        target[0].T,
        returned[0].T,
        cache[0],
        enc_weight[0],
        weights,
    )
    return (err.T[None], jnp.transpose(out, (1, 2, 0)), grad[None])


def solution(mesh):
    placed = (
        P("section", None, None),
        P(),
        P("section", ("dp", "tensor"), None),
        P("section", ("dp", "tensor")),
        P("section", None, ("dp", "tensor"), None),
        P("section", ("dp", "tensor")),
        P("section", None, ("dp", "tensor")),
        P("section", None, ("dp", "tensor")),
        P("section", None, ("dp", "tensor")),
    )
    return jax.shard_map(
        local,
        mesh=mesh,
        in_specs=placed,
        out_specs=(
            P("section", None, ("dp", "tensor")),
            P("section", None, ("dp", "tensor")),
            P("section", ("dp", "tensor"), None),
        ),
        check_vma=False,
    )
```

time: 2310 us -> 112 us (0.05)
  waiting for transfers between devices: 1920 us -> 0 us
  starting transfers between devices: 339 us -> 0 us
  Pallas kernels: 0 us -> 101 us
    unnamed x3 -> x0, waiting for transfers between devices: 1340 us -> none
    ppermute x28 -> x0, waiting for transfers between devices: 346 us -> none  [passed_along(): return lax.ppermute(shard, axis, pairs)]
    ppermute x28 -> x0, starting transfers between devices: 339 us -> none  [passed_along(): return lax.ppermute(shard, axis, pairs)]
    all_gather x1 -> x0, waiting for transfers between devices: 242 us -> none  [local(): lax.all_gather(latents, ('dp', 'tensor'), axis=1, tiled=True)]
    pallas_call x0 -> x1, Pallas kernels: none -> 101 us  [local(): pl.pallas_call(kernel, out_shape=(jax.ShapeDtypeStruct((21, 128), BF16),...]
  transfers between devices with their start and end apart: 30 -> 0, of which waited for: 29 -> 0; matrix products, arithmetic and copies ran while one was open for 0% -> 0% of each run, Pallas kernels for 0% -> 0%
where the time goes in v1:
time: 112 us; the launch traced here: 110 us
  Pallas kernels  101 us (90%)
  local copies, waits for them, and re-layouts  8.73 us (8%)
    pallas_call x1, Pallas kernels, local(): pl.pallas_call(kernel, out_shape=(jax.ShapeDtypeStruct((21, 128), BF16),...  101 us
    unnamed x19, local copies, waits for them, and re-layouts  8.73 us

profile of v1, /device:TPU:24, one launch (start us, length us, event | category | flops | bytes accessed | tf_op | source)
XLA Modules:
  0.0 110.4 jit_solution(13059460551558016568)
XLA Ops:
  0.6 0.0 copy-start
  0.6 1.8 %copy-done = bf16[1,256,5376]{2,1,0:T(8,128)(2,1)S(1)} copy-done((bf16[1,256,5376]{2,1,0:T(8,128)(2,1)S(1)}, bf16[1,256,5376]{2,1,0:T(8,128)(2,1)}, u32[]{:S(2)}) %copy-start) | copy-done | bytes 2752536
  2.4 0.0 copy-start.1
  2.4 1.1 copy-done.1
  3.5 0.0 copy-start.2
  3.5 0.7 copy-done.2
  4.2 0.0 copy-start.3
  4.2 0.7 copy-done.3
  4.9 0.0 copy-start.4
  4.9 0.7 copy-done.4
  5.6 0.0 copy-start.5
  5.6 0.7 copy-done.5
  6.3 0.0 copy-start.6
  6.3 0.7 copy-done.6
  6.9 0.0 copy-start.7
  6.9 0.7 copy-done.7
  7.6 101.1 %transcoder.1 = (bf16[21,128]{1,0:T(8,128)(2,1)S(1)}, f32[21,1,128]{2,1,0:T(1,128)S(1)}, f32[64,128]{1,0:T(8,128)S(1)}) custom-call(s32[1,128]{1,0:T(1,128)S(1)} %bitcast.28, f32[1,64]{1,0:T(1,128)S(1)} %copy-done.6, f32[1,21]{1,0:T(1,128)S(1)} %copy-done.7, f32[21,1,128]{2,1,0:T(1,128)S(1)} %bitcast.23, bf16[21,128]{1,0:T(8,128)(2,1)S(1)} %bitcast.25, ...), custom_call_target="tpu_custom_call" | custom-call | tf_op jit(solution)/shard_map/transcoder/pallas_call | solution.py:301
  108.6 0.6 copy.15
  109.2 0.6 copy.16
  109.8 0.6 copy.17
Async XLA Ops:
  0.6 1.8 %copy-start = (bf16[1,256,5376]{2,1,0:T(8,128)(2,1)S(1)}, bf16[1,256,5376]{2,1,0:T(8,128)(2,1)}, u32[]{:S(2)}) copy-start(bf16[1,256,5376]{2,1,0:T(8,128)(2,1)} %param.9) | copy-start | bytes 8257540
  2.4 1.1 copy-start.1
  3.5 0.7 copy-start.2
  4.2 0.7 copy-start.3
  4.9 0.7 copy-start.4
  5.6 0.7 copy-start.5
  6.3 0.7 copy-start.6
  6.9 0.7 copy-start.7

commit v2 on v1

v2 whole, which is shorter than its diff:
```python
import jax
import jax.numpy as jnp
from jax import lax
from jax.experimental import pallas as pl
from jax.experimental.pallas import tpu as pltpu
from jax.sharding import PartitionSpec as P

MESH = pl.DeviceIdType.MESH
F32 = jnp.float32
BF16 = jnp.bfloat16
FEAT = 24
ORDER = (1, 3, 2)


class Links:
    def __init__(self, send, recv):
        self.send, self.recv, self.used, self.open = send, recv, 0, []

    def message(self):
        self.used += 1
        return self.used - 1

    def copy(self, index, src, dst, peer, lands=None):
        return pltpu.make_async_remote_copy(
            src_ref=src,
            dst_ref=dst,
            send_sem=self.send.at[index],
            recv_sem=self.recv.at[index if lands is None else lands],
            device_id=peer,
            device_id_type=MESH,
        )

    def start(self, index, src, dst, peer, lands=None):
        copy = self.copy(index, src, dst, peer, lands)
        copy.start()
        self.open.append(copy)

    def arrived(self, index, dst, peer):
        self.copy(index, dst, dst, peer).wait_recv()

    def drain(self):
        for copy in self.open:
            copy.wait_send()


MESSAGES = 112


def column_of(row, rows):
    n = row.shape[1]
    down = lax.broadcasted_iota(jnp.int32, (rows, n), 0)
    along = lax.broadcasted_iota(jnp.int32, (rows, n), 1)
    return jnp.sum(jnp.where(down == along, row, 0.0), axis=1, keepdims=True)


def kernel(
    tok_h, ebias_h, dbias_h, inc_h, tgt_h, ret_h, cache_h, enc_h, w_h,
    err_o, out_o, lg_o, tok, ebias, dbias, inc, tgt, ret,
    cache_v, enc_v, w_v, lat, pbuf, rc, qbuf, rx, ub, rb, vf, vb, ra,
    cacc, bk, ysend, yrecv, zsend, zrecv, osend, orecv, esend, erecv,
    rsend, rrecv, gsend, grecv, load, send, recv,
):
    s, d, t = lax.axis_index("section"), lax.axis_index("dp"), lax.axis_index("tensor")
    y, zh, x, z, c = s // 2, s % 2, d, t // 2, t % 2
    zg, zp = z // 4, z % 4
    core_peer = (s, d, z * 2 + 1 - c)
    x_peer = lambda k: (s, (x + k) % 4, t)
    a_peer = lambda at: (s, d, (at * 4 + zp) * 2 + c)
    b_peer = lambda k: (s, d, (zg * 4 + (zp + k) % 4) * 2 + c)
    y_peer = lambda k: (((y + k) % 4) * 2 + zh, d, t)
    z_peer = (y * 2 + 1 - zh, d, t)

    barrier = pltpu.get_barrier_semaphore()
    peers = [z_peer, core_peer]
    for k in (1, 2, 3):
        peers += [a_peer((zg + k) % 4), b_peer(k), x_peer(k), y_peer(k)]
    for peer in peers:
        pl.semaphore_signal(barrier, inc=1, device_id=peer, device_id_type=MESH)

    pairs = (
        (cache_h, cache_v), (enc_h, enc_v), (tok_h, tok), (ebias_h, ebias), (ret_h, ret),
        (w_h, w_v), (dbias_h, dbias), (inc_h, inc), (tgt_h, tgt),
    )
    loads = [
        pltpu.make_async_copy(src, dst, load.at[i]) for i, (src, dst) in enumerate(pairs)
    ]
    for one in loads:
        one.start()
    links = Links(send, recv)

    loads[2].wait()
    loads[3].wait()
    rows_of = lax.broadcasted_iota(jnp.int32, (256, 128), 0)
    pick = jnp.where(rows_of == tok[...], 1.0, 0.0).astype(BF16)
    bias = column_of(ebias[...], 64)
    loads[0].wait()
    loads[1].wait()
    pre = lax.dot_general(
        enc_v[...], cache_v[...], (((1,), (1,)), ((), ())), preferred_element_type=F32
    )
    every = jnp.maximum(pre + bias, 0.0).astype(BF16)
    mine = jnp.dot(every, pick, preferred_element_type=F32).astype(BF16)
    lat[x, zg, zp, c] = mine

    pl.semaphore_wait(barrier, len(peers))

    zone = (zg, zg + 1 - 2 * (zg % 2), 2 - zg // 2, 3 - 3 * (zg // 2))
    m_a = {i: links.message() for i in range(4)}
    m_b = {(k, i): links.message() for k in (1, 2, 3) for i in range(4)}
    m_x = {(k, i): links.message() for k in (1, 2, 3) for i in range(4)}
    m_c = {(k, i): links.message() for k in range(4) for i in range(4)}
    own = lat.at[x, zg, zp, c]
    for i in (3, 2, 1):
        links.start(m_a[i], own, own, a_peer(zone[i]), m_a[0] + zg)

    def spread(i):
        chunk = lat.at[x, zone[i], zp, c]
        for k in ORDER:
            links.start(m_b[k, i], chunk, chunk, b_peer(k))

    def from_far(i):
        links.arrived(m_a[0] + zone[i], lat.at[x, zone[i], zp, c], a_peer(zone[i]))
        spread(i)

    def group(k, i):
        return lat.at[(x - k + 4) % 4, zone[i], :, c]

    def to_core(k, i):
        links.start(m_c[k, i], group(k, i), group(k, i), core_peer)

    def from_group(i):
        for k in ORDER:
            links.arrived(m_b[k, i], lat.at[x, zone[i], (zp - k + 4) % 4, c], b_peer(k))
        for k in (2, 1, 3):
            links.start(m_x[k, i], group(0, i), group(0, i), x_peer(k))
        to_core(0, i)

    def from_x(i):
        for k in ORDER:
            links.arrived(m_x[k, i], group(k, i), x_peer(k))
            to_core(k, i)

    def weights(x_at, zg_at):
        first = pl.multiple_of((x_at * 4 + zg_at) * 512, 512)
        return w_v[:, pl.ds(first, 512)]

    def decode(k, i):
        x_at = (x - k + 4) % 4
        links.arrived(m_c[k, i], lat.at[x_at, zone[i], :, 1 - c], core_peer)
        block = lat[x_at, zone[i]].reshape(512, 128)
        cacc[0:168] += jnp.dot(weights(x_at, zone[i]), block, preferred_element_type=F32)

    spread(0)

    loads[4].wait()
    zero_rows = jnp.zeros((FEAT - 21, 128), F32)
    returned = jnp.concatenate([ret[...].astype(F32), zero_rows], axis=0)
    rsend[...] = jnp.concatenate([returned, jnp.zeros((8, 128), F32)], axis=0).astype(BF16)
    m_r = links.message()
    links.start(m_r, rsend, rrecv, z_peer)

    cacc[...] = jnp.zeros_like(cacc)
    for one in loads[5:]:
        one.wait()
    from_group(0)
    from_far(1)
    from_far(2)
    from_group(1)
    from_x(0)
    from_far(3)
    from_group(2)
    from_x(1)
    for k in range(4):
        decode(k, 0)
    from_group(3)
    from_x(2)
    for k in range(4):
        decode(k, 1)
    decode(0, 2)
    from_x(3)

    links.arrived(m_r, rrecv, z_peer)
    gsend[...] = jnp.concatenate([returned, rrecv[...].astype(F32)[:FEAT]], axis=0).astype(BF16)
    m_g = {k: links.message() for k in (1, 2, 3)}
    for k in ORDER:
        links.start(m_g[k], gsend, grecv.at[k - 1], y_peer(k))
    for k in ORDER:
        decode(k, 2)
    for k in range(4):
        decode(k, 3)

    def piece(offset):
        return cacc[pl.ds(offset, FEAT, stride=8), :]

    cross_of = lambda dy: (2 * dy + 1 - 2 * zh + 8) % 8
    m_y = {k: links.message() for k in (1, 2, 3)}
    for k in ORDER:
        ysend[k - 1] = jnp.concatenate([piece(2 * k), piece(cross_of(k))], axis=0).astype(BF16)
        links.start(m_y[k], ysend.at[k - 1], yrecv.at[k - 1], y_peer(k))
    base = inc[...].reshape(21, 128) + column_of(dbias[...], 21) - tgt[...].astype(F32)
    base = jnp.concatenate([base, zero_rows], axis=0)
    own_cross = piece(cross_of(0))
    e_same = base + piece(0)
    o_same = jnp.zeros((FEAT, 128), F32)
    e_cross = jnp.where(zh == 0, own_cross, 0.0)
    o_cross = jnp.where(zh == 0, 0.0, own_cross)
    for k in ORDER:
        links.arrived(m_y[k], yrecv.at[k - 1], y_peer(k))
        both = yrecv[k - 1].astype(F32)
        same, cross = both[:FEAT], both[FEAT:]
        e_same += jnp.where(y >= k, same, 0.0)
        o_same += jnp.where(y >= k, 0.0, same)
        e_cross += jnp.where(y >= k, cross, 0.0)
        o_cross += jnp.where(y >= k, 0.0, cross)
    m_z, m_o = links.message(), links.message()
    zsend[...] = jnp.concatenate([e_same, e_cross], axis=0).astype(BF16)
    links.start(m_z, zsend, zrecv, z_peer)
    osend[...] = jnp.concatenate([o_cross, jnp.zeros((8, 128), F32)], axis=0).astype(BF16)
    links.arrived(m_z, zrecv, z_peer)
    both = zrecv[...].astype(F32)
    mine_err = e_same + both[FEAT:]
    other_err = e_cross + both[:FEAT]
    esend[...] = jnp.concatenate([mine_err, other_err], axis=0).astype(BF16)
    m_e = {k: links.message() for k in (1, 2, 3)}
    for k in ORDER:
        links.start(m_e[k], esend, erecv.at[k - 1], y_peer(k))
    links.start(m_o, osend, orecv, z_peer)
    err_o[...] = mine_err[:21].astype(BF16)

    for dy in range(4):
        k = (4 - dy) % 4
        if k == 0:
            mine_b, ret_b = esend[...].astype(F32), gsend[...].astype(F32)
            same = mine_b[:FEAT]
            cross = jnp.where(zh == 0, mine_b[FEAT:], ret_b[FEAT:])
        else:
            links.arrived(m_g[k], grecv.at[k - 1], y_peer(k))
            links.arrived(m_e[k], erecv.at[k - 1], y_peer(k))
            mine_b, ret_b = erecv[k - 1].astype(F32), grecv[k - 1].astype(F32)
            both = jnp.where(y + dy < 4, mine_b, ret_b)
            same, cross = both[:FEAT], both[FEAT:]
        bk[pl.ds(2 * dy, FEAT, stride=8), :] = same
        bk[pl.ds(cross_of(dy), FEAT, stride=8), :] = cross
    back = bk[0:168].astype(BF16)

    n_c = {(k, i): links.message() for k in range(4) for i in range(4)}
    n_x = {(k, i): links.message() for k in (1, 2, 3) for i in range(4)}
    n_b = {(k, i): links.message() for k in (1, 2, 3) for i in range(4)}
    n_a = {i: links.message() for i in range(4)}

    def gradient(k, i):
        x_at = (x + k) % 4
        part = lax.dot_general(
            weights(x_at, zone[i]), back, (((0,), (0,)), ((), ())), preferred_element_type=F32
        )
        pbuf[x_at, zone[i]] = part.astype(BF16).reshape(4, 2, 64, 128)
        links.start(n_c[k, i], pbuf.at[x_at, zone[i], :, 1 - c], rc.at[k, i], core_peer)

    def chip_sum(k, i):
        links.arrived(n_c[k, i], rc.at[k, i], core_peer)
        total = pbuf[(x + k) % 4, zone[i], :, c].astype(F32) + rc[k, i].astype(F32)
        qbuf[k, i] = total.astype(BF16)
        if k > 0:
            links.start(n_x[k, i], qbuf.at[k, i], rx.at[k - 1, i], x_peer(k))

    def row_sum(i):
        total = qbuf[0, i].astype(F32)
        for k in ORDER:
            links.arrived(n_x[k, i], rx.at[k - 1, i], x_peer(k))
            total += rx[k - 1, i].astype(F32)
        ub[i] = total.astype(BF16)
        vf[i] = total
        for k in ORDER:
            links.start(n_b[k, i], ub.at[i, (zp + k) % 4], rb.at[i, k - 1], b_peer(k))

    def group_sum(i):
        total = vf[i, zp]
        for k in ORDER:
            links.arrived(n_b[k, i], rb.at[i, k - 1], b_peer(k))
            total += rb[i, k - 1].astype(F32)
        if i > 0:
            vb[i - 1] = total.astype(BF16)
            links.start(n_a[i], vb.at[i - 1], ra.at[zg], a_peer(zone[i]), n_a[0] + zg)
        return total

    steps = [(k, i) for i in (3, 2, 1, 0) for k in (2, 1, 3, 0)]
    for at, step in enumerate(steps):
        if at == 12:
            row_sum(3)
        gradient(*step)
        if at >= 2:
            chip_sum(*steps[at - 2])
    chip_sum(*steps[-2])
    chip_sum(*steps[-1])
    row_sum(2)
    group_sum(3)
    row_sum(1)
    group_sum(2)
    links.arrived(m_o, orecv, z_peer)
    outgoing = o_same + orecv[...].astype(F32)[:FEAT]
    out_o[...] = outgoing[:21].reshape(21, 1, 128)
    row_sum(0)
    group_sum(1)
    total = group_sum(0)
    for i in (3, 2, 1):
        links.arrived(n_a[0] + zone[i], ra.at[zone[i]], a_peer(zone[i]))
        total += ra[zone[i]].astype(F32)
    lg_o[...] = total
    links.drain()


def local(cache, token_ids, enc_weight, enc_bias, dec_weight, dec_bias, incoming, target, returned):
    whole = pl.BlockSpec(memory_space=pltpu.VMEM)
    left = pl.BlockSpec(memory_space=pltpu.HBM)
    weights = jnp.transpose(dec_weight[0], (1, 0, 2)).reshape(168, 8192)
    err, out, grad = pl.pallas_call(
        kernel,
        out_shape=(
            jax.ShapeDtypeStruct((21, 128), BF16),
            jax.ShapeDtypeStruct((21, 1, 128), F32),
            jax.ShapeDtypeStruct((64, 128), F32),
        ),
        in_specs=[left] * 9,
        out_specs=(whole, whole, whole),
        scratch_shapes=[
            pltpu.VMEM((1, 128), jnp.int32),
            pltpu.VMEM((1, 64), F32),
            pltpu.VMEM((1, 21), F32),
            pltpu.VMEM((21, 1, 128), F32),
            pltpu.VMEM((21, 128), BF16),
            pltpu.VMEM((21, 128), BF16),
            pltpu.VMEM((256, 5376), BF16),
            pltpu.VMEM((64, 5376), BF16),
            pltpu.VMEM((168, 8192), BF16),
            pltpu.VMEM((4, 4, 4, 2, 64, 128), BF16),
            pltpu.VMEM((4, 4, 4, 2, 64, 128), BF16),
            pltpu.VMEM((4, 4, 4, 64, 128), BF16),
            pltpu.VMEM((4, 4, 4, 64, 128), BF16),
            pltpu.VMEM((3, 4, 4, 64, 128), BF16),
            pltpu.VMEM((4, 4, 64, 128), BF16),
            pltpu.VMEM((4, 3, 64, 128), BF16),
            pltpu.VMEM((4, 4, 64, 128), F32),
            pltpu.VMEM((3, 64, 128), BF16),
            pltpu.VMEM((4, 64, 128), BF16),
            pltpu.VMEM((192, 128), F32),
            pltpu.VMEM((192, 128), F32),
            pltpu.VMEM((3, 48, 128), BF16),
            pltpu.VMEM((3, 48, 128), BF16),
            pltpu.VMEM((48, 128), BF16),
            pltpu.VMEM((48, 128), BF16),
            pltpu.VMEM((32, 128), BF16),
            pltpu.VMEM((32, 128), BF16),
            pltpu.VMEM((48, 128), BF16),
            pltpu.VMEM((3, 48, 128), BF16),
            pltpu.VMEM((32, 128), BF16),
            pltpu.VMEM((32, 128), BF16),
            pltpu.VMEM((48, 128), BF16),
            pltpu.VMEM((3, 48, 128), BF16),
            pltpu.SemaphoreType.DMA((9,)),
            pltpu.SemaphoreType.DMA((MESSAGES,)),
            pltpu.SemaphoreType.DMA((MESSAGES,)),
        ],
        compiler_params=pltpu.CompilerParams(
            collective_id=0, has_side_effects=True, vmem_limit_bytes=64 << 20
        ),
        name="transcoder",
    )(
        token_ids.reshape(1, 128),
        enc_bias,
        dec_bias,
        jnp.transpose(incoming, (2, 0, 1)),
        target[0].T,
        returned[0].T,
        cache[0],
        enc_weight[0],
        weights,
    )
    return (err.T[None], jnp.transpose(out, (1, 2, 0)), grad[None])


def solution(mesh):
    placed = (
        P("section", None, None),
        P(),
        P("section", ("dp", "tensor"), None),
        P("section", ("dp", "tensor")),
        P("section", None, ("dp", "tensor"), None),
        P("section", ("dp", "tensor")),
        P("section", None, ("dp", "tensor")),
        P("section", None, ("dp", "tensor")),
        P("section", None, ("dp", "tensor")),
    )
    return jax.shard_map(
        local,
        mesh=mesh,
        in_specs=placed,
        out_specs=(
            P("section", None, ("dp", "tensor")),
            P("section", None, ("dp", "tensor")),
            P("section", ("dp", "tensor"), None),
        ),
        check_vma=False,
    )
```

time: 112 us -> 98.4 us (0.88)
  the two profiles are of different devices: /device:TPU:24 before, /device:TPU:64 now
where the time goes in v2:
time: 98.4 us; the launch traced here: 98.2 us
  Pallas kernels  93.5 us (95%)
  local copies, waits for them, and re-layouts  3.96 us (4%)
    pallas_call x1, Pallas kernels, local(): pl.pallas_call(kernel, out_shape=(jax.ShapeDtypeStruct((21, 128), BF16),...  93.5 us
    unnamed x3, local copies, waits for them, and re-layouts  3.96 us

profile of v2, /device:TPU:64, one launch (start us, length us, event | category | flops | bytes accessed | tf_op | source)
XLA Modules:
  0.0 98.2 jit_solution(4585253987071070395)
XLA Ops:
  0.6 93.5 %transcoder.1 = (bf16[21,128]{1,0:T(8,128)(2,1)}, f32[21,1,128]{2,1,0:T(1,128)}, f32[64,128]{1,0:T(8,128)}) custom-call(s32[1,128]{1,0:T(1,128)} %bitcast.29, f32[1,64]{1,0:T(1,128)} %ebias_h.1, f32[1,21]{1,0:T(1,128)} %dbias_h.1, f32[21,1,128]{2,1,0:T(1,128)} %bitcast.24, bf16[21,128]{1,0:T(8,128)(2,1)} %bitcast.26, bf16[21,128]{1,0:T(8,128)(2,1)} %bitcast.27, ...), custom_call_target="tpu_custom_call" | custom-call | tf_op jit(solution)/shard_map/transcoder/pallas_call | solution.py:316
  94.2 1.3 %copy.15 = bf16[1,128,21]{1,2,0:T(8,128)(2,1)} copy(bf16[1,128,21]{1,2,0:T(8,128)(2,1)} %bitcast.28) | data formatting | bytes 10752
  95.5 1.3 %copy.16 = f32[1,128,21]{1,0,2:T(1,128)} copy(f32[1,128,21]{1,0,2:T(1,128)} %bitcast.25) | data formatting | bytes 21504
  96.8 1.4 %copy.17 = f32[1,64,128]{2,1,0:T(8,128)} copy(f32[1,64,128]{2,1,0:T(8,128)} %bitcast.23) | data formatting | bytes 65536

commit v3 on v2

--- a/solution.py
+++ b/solution.py
@@ -44,6 +44,7 @@
 
 
 MESSAGES = 112
+LAG = 9
 
 
 def column_of(row, rows):
@@ -152,15 +153,8 @@
 
     spread(0)
 
-    loads[4].wait()
-    zero_rows = jnp.zeros((FEAT - 21, 128), F32)
-    returned = jnp.concatenate([ret[...].astype(F32), zero_rows], axis=0)
-    rsend[...] = jnp.concatenate([returned, jnp.zeros((8, 128), F32)], axis=0).astype(BF16)
-    m_r = links.message()
-    links.start(m_r, rsend, rrecv, z_peer)
-
     cacc[...] = jnp.zeros_like(cacc)
-    for one in loads[5:]:
+    for one in loads[4:]:
         one.wait()
     from_group(0)
     from_far(1)
@@ -173,17 +167,19 @@
     for k in range(4):
         decode(k, 0)
     from_group(3)
+
+    zero_rows = jnp.zeros((FEAT - 21, 128), F32)
+    returned = jnp.concatenate([ret[...].astype(F32), zero_rows], axis=0)
+    rsend[...] = jnp.concatenate([returned, jnp.zeros((8, 128), F32)], axis=0).astype(BF16)
+    m_r = links.message()
+    links.start(m_r, rsend, rrecv, z_peer)
+
     from_x(2)
     for k in range(4):
         decode(k, 1)
     decode(0, 2)
     from_x(3)
 
-    links.arrived(m_r, rrecv, z_peer)
-    gsend[...] = jnp.concatenate([returned, rrecv[...].astype(F32)[:FEAT]], axis=0).astype(BF16)
-    m_g = {k: links.message() for k in (1, 2, 3)}
-    for k in ORDER:
-        links.start(m_g[k], gsend, grecv.at[k - 1], y_peer(k))
     for k in ORDER:
         decode(k, 2)
     for k in range(4):
@@ -216,6 +212,13 @@
     zsend[...] = jnp.concatenate([e_same, e_cross], axis=0).astype(BF16)
     links.start(m_z, zsend, zrecv, z_peer)
     osend[...] = jnp.concatenate([o_cross, jnp.zeros((8, 128), F32)], axis=0).astype(BF16)
+
+    links.arrived(m_r, rrecv, z_peer)
+    gsend[...] = jnp.concatenate([returned, rrecv[...].astype(F32)[:FEAT]], axis=0).astype(BF16)
+    m_g = {k: links.message() for k in (1, 2, 3)}
+    for k in ORDER:
+        links.start(m_g[k], gsend, grecv.at[k - 1], y_peer(k))
+
     links.arrived(m_z, zrecv, z_peer)
     both = zrecv[...].astype(F32)
     mine_err = e_same + both[FEAT:]
@@ -284,14 +287,12 @@
         return total
 
     steps = [(k, i) for i in (3, 2, 1, 0) for k in (2, 1, 3, 0)]
-    for at, step in enumerate(steps):
-        if at == 12:
-            row_sum(3)
-        gradient(*step)
-        if at >= 2:
-            chip_sum(*steps[at - 2])
-    chip_sum(*steps[-2])
-    chip_sum(*steps[-1])
+    for at in range(len(steps) + LAG):
+        if at < len(steps):
+            gradient(*steps[at])
+        if at >= LAG:
+            chip_sum(*steps[at - LAG])
+    row_sum(3)
     row_sum(2)
     group_sum(3)
     row_sum(1)
@@ -309,17 +310,26 @@
     links.drain()
 
 
+def hand_over(*refs):
+    moves = [pltpu.make_async_copy(refs[i], refs[i + 3], refs[6].at[i]) for i in range(3)]
+    for move in moves:
+        move.start()
+    for move in moves:
+        move.wait()
+
+
 def local(cache, token_ids, enc_weight, enc_bias, dec_weight, dec_bias, incoming, target, returned):
     whole = pl.BlockSpec(memory_space=pltpu.VMEM)
     left = pl.BlockSpec(memory_space=pltpu.HBM)
     weights = jnp.transpose(dec_weight[0], (1, 0, 2)).reshape(168, 8192)
-    err, out, grad = pl.pallas_call(
+    shapes = (
+        jax.ShapeDtypeStruct((21, 128), BF16),
+        jax.ShapeDtypeStruct((21, 1, 128), F32),
+        jax.ShapeDtypeStruct((64, 128), F32),
+    )
+    results = pl.pallas_call(
         kernel,
-        out_shape=(
-            jax.ShapeDtypeStruct((21, 128), BF16),
-            jax.ShapeDtypeStruct((21, 1, 128), F32),
-            jax.ShapeDtypeStruct((64, 128), F32),
-        ),
+        out_shape=shapes,
         in_specs=[left] * 9,
         out_specs=(whole, whole, whole),
         scratch_shapes=[
@@ -375,6 +385,15 @@
         enc_weight[0],
         weights,
     )
+    err, out, grad = pl.pallas_call(
+        hand_over,
+        out_shape=shapes,
+        in_specs=[left] * 3,
+        out_specs=(left, left, left),
+        scratch_shapes=[pltpu.SemaphoreType.DMA((3,))],
+        compiler_params=pltpu.CompilerParams(vmem_limit_bytes=64 << 20),
+        name="results",
+    )(*results)
     return (err.T[None], jnp.transpose(out, (1, 2, 0)), grad[None])
 
 

time: 98.4 us -> 97.5 us (level)
  the two profiles are of different devices: /device:TPU:64 before, /device:TPU:24 now
where the time goes in v3:
time: 97.5 us; the launch traced here: 97.1 us
  Pallas kernels  96.5 us (99%)
    pallas_call x1, Pallas kernels, local(): pl.pallas_call(kernel, out_shape=shapes, in_specs=[left] * 9, out_specs=(...  93.9 us
    pallas_call x1, Pallas kernels, local(): pl.pallas_call(hand_over, out_shape=shapes, in_specs=[left] * 3, out_spec...  2.63 us

profile of v3, /device:TPU:24, one launch (start us, length us, event | category | flops | bytes accessed | tf_op | source)
XLA Modules:
  0.0 97.1 jit_solution(9480579785601201001)
XLA Ops:
  0.6 93.9 %transcoder.1 = (bf16[21,128]{1,0:T(8,128)(2,1)}, f32[21,1,128]{2,1,0:T(1,128)}, f32[64,128]{1,0:T(8,128)}) custom-call(s32[1,128]{1,0:T(1,128)} %bitcast.26, f32[1,64]{1,0:T(1,128)} %ebias_h.1, f32[1,21]{1,0:T(1,128)} %dbias_h.1, f32[21,1,128]{2,1,0:T(1,128)} %bitcast.23, bf16[21,128]{1,0:T(8,128)(2,1)} %bitcast.24, bf16[21,128]{1,0:T(8,128)(2,1)} %bitcast.25, ...), custom_call_target="tpu_custom_call" | custom-call | tf_op jit(solution)/shard_map/transcoder/pallas_call | solution.py:330
  94.5 2.6 %results.1 = (bf16[21,128]{1,0:T(8,128)(2,1)}, f32[21,1,128]{2,1,0:T(1,128)}, f32[64,128]{1,0:T(8,128)}) custom-call(bf16[21,128]{1,0:T(8,128)(2,1)} %get-tuple-element.9.refs_0_, f32[21,1,128]{2,1,0:T(1,128)} %get-tuple-element.10.refs_1_, f32[64,128]{1,0:T(8,128)} %get-tuple-element.11.refs_2_), custom_call_target="tpu_custom_call" | custom-call | tf_op jit(solution)/shard_map/results/pallas_call | solution.py:388

commit v4 on v3

--- a/solution.py
+++ b/solution.py
@@ -292,7 +292,8 @@
             gradient(*steps[at])
         if at >= LAG:
             chip_sum(*steps[at - LAG])
-    row_sum(3)
+        if at == 11 + LAG:
+            row_sum(3)
     row_sum(2)
     group_sum(3)
     row_sum(1)

time: 97.5 us -> 97.3 us (level)
  no operation moved by 1% of the time
where the time goes in v4:
time: 97.3 us; the launch traced here: 97.1 us
  Pallas kernels  96.5 us (99%)
    pallas_call x1, Pallas kernels, local(): pl.pallas_call(kernel, out_shape=shapes, in_specs=[left] * 9, out_specs=(...  93.9 us
    pallas_call x1, Pallas kernels, local(): pl.pallas_call(hand_over, out_shape=shapes, in_specs=[left] * 3, out_spec...  2.63 us

profile of v4, /device:TPU:24, one launch (start us, length us, event | category | flops | bytes accessed | tf_op | source)
XLA Modules:
  0.0 97.1 jit_solution(3482336340271643297)
XLA Ops:
  0.6 93.9 %transcoder.1 = (bf16[21,128]{1,0:T(8,128)(2,1)}, f32[21,1,128]{2,1,0:T(1,128)}, f32[64,128]{1,0:T(8,128)}) custom-call(s32[1,128]{1,0:T(1,128)} %bitcast.26, f32[1,64]{1,0:T(1,128)} %ebias_h.1, f32[1,21]{1,0:T(1,128)} %dbias_h.1, f32[21,1,128]{2,1,0:T(1,128)} %bitcast.23, bf16[21,128]{1,0:T(8,128)(2,1)} %bitcast.24, bf16[21,128]{1,0:T(8,128)(2,1)} %bitcast.25, ...), custom_call_target="tpu_custom_call" | custom-call | tf_op jit(solution)/shard_map/transcoder/pallas_call | solution.py:331
  94.5 2.6 %results.1 = (bf16[21,128]{1,0:T(8,128)(2,1)}, f32[21,1,128]{2,1,0:T(1,128)}, f32[64,128]{1,0:T(8,128)}) custom-call(bf16[21,128]{1,0:T(8,128)(2,1)} %get-tuple-element.9.refs_0_, f32[21,1,128]{2,1,0:T(1,128)} %get-tuple-element.10.refs_1_, f32[64,128]{1,0:T(8,128)} %get-tuple-element.11.refs_2_), custom_call_target="tpu_custom_call" | custom-call | tf_op jit(solution)/shard_map/results/pallas_call | solution.py:389
